TPU v7x, 512 devices: a whole 4x4x16 slice. The times are simulated.
512 devices in a mesh: vocab: 16 (over z_hi, x, core), seq: 32 (over z_lo, y).
Axes of the slice: x: 4, y: 4, z: 16 (z_hi: 2, z_lo: 8; z = z_hi * 8 + z_lo), core: 2. Of those that a mesh axis runs over, the one named last changes fastest.
Arguments:
- token_ids: int32 [2, 2048], P(None, 'seq'), may hold values from 0 to 131071
- keep_mask: int32 [2, 2048], P(None, 'seq'), may hold values 0 or 1
- target_length: int32 [2], replicated, may hold values from 256 to 2048, as said below
- source_length: int32 [2], replicated, may hold values from 128 to 1024, as said below
- embed_table: bfloat16 [131072, 4096], P('vocab', 'seq'), may hold values from -6 to 6
- self_gain: float32 [4096], replicated, may hold values from 0.1 to 1.9
- query_weight: bfloat16 [4096, 2048], P('seq', 'vocab'), may hold values from -0.03125 to 0.03125
- key_weight: bfloat16 [4096, 2048], P('seq', 'vocab'), may hold values from -6 to 6
- value_weight: bfloat16 [4096, 2048], P('seq', 'vocab'), may hold values from -0.09375 to 0.09375
- self_out_weight: bfloat16 [2048, 4096], P('vocab'), may hold values from -0.5 to 0.5
- cross_gain: float32 [4096], replicated, may hold values from 0.1 to 1.9
- cross_query_weight: bfloat16 [4096, 2048], P('seq', 'vocab'), may hold values from -0.03125 to 0.03125
- cross_keys: bfloat16 [2, 1024, 2048], P(None, 'seq', 'vocab'), may hold values from -24 to 24
- cross_values: bfloat16 [2, 1024, 2048], P(None, 'seq', 'vocab'), may hold values from -6 to 6
- cross_out_weight: bfloat16 [2048, 4096], P('vocab'), may hold values from -0.375 to 0.375
Outputs:
- layer_output: bfloat16 [2, 2048, 4096], P(None, 'seq', 'vocab')
Inputs may be any that keep to these rules, and one draw needn't show every extreme that they name: `target_length`: the pairs' lengths all differ, and one pair has length 2048. `source_length`: the pairs' lengths all differ, and one pair has length 1024.
All inputs are finite; a program needn't handle non-finite values. No bound on the sum of `keep_mask` on one device may be relied on, other than what follows from the above.
Results may differ from a plain program's by a relative error of at most 0.035.
Values may be sent and summed in bfloat16 or wider, within the bound.
A program may use at most 64 MiB of HBM per device.

v0:
```python
import jax
import jax.numpy as jnp
from jax import lax
from jax.sharding import PartitionSpec as P

DH = 64


def rms_scale(values, gain):
    return values * lax.rsqrt(jnp.mean(values * values, axis=-1, keepdims=True) + 1e-06) * gain


def attend(query, keys, values, visible):
    pair_count = query.shape[0]
    query_rows = query.shape[1]
    head_count = query.shape[2] // DH
    q_heads = query.reshape(pair_count, query_rows, head_count, DH)
    k_heads = keys.reshape(pair_count, keys.shape[1], head_count, DH)
    v_heads = values.reshape(pair_count, values.shape[1], head_count, DH)
    scores = jnp.einsum("pqhd,pkhd->phqk", q_heads, k_heads, preferred_element_type=jnp.float32)
    scores = jnp.where(visible[:, None, :, :], scores, -jnp.inf)
    raised = jnp.exp(scores - jnp.max(scores, axis=-1, keepdims=True))
    totals = jnp.sum(raised, axis=-1)
    mixed = jnp.einsum(
        "phqk,pkhd->pqhd", raised.astype(jnp.bfloat16), v_heads, preferred_element_type=jnp.float32
    )
    mixed = mixed / jnp.transpose(totals, (0, 2, 1))[:, :, :, None]
    return mixed.reshape(pair_count, query_rows, head_count * DH).astype(jnp.bfloat16)


def row_fold(source, portion):
    return jnp.dot(source, portion, preferred_element_type=jnp.float32)


def on_device(
    token_ids,
    keep_mask,
    target_length,
    source_length,
    embed_table,
    self_gain,
    query_weight,
    key_weight,
    value_weight,
    self_out_weight,
    cross_gain,
    cross_query_weight,
    cross_keys,
    cross_values,
    cross_out_weight,
):
    seq_count = lax.axis_size("seq")
    seq_index = lax.axis_index("seq")
    vocab_index = lax.axis_index("vocab")
    vocab_count = lax.axis_size("vocab")
    every_id = lax.all_gather(token_ids, "seq", axis=1, tiled=True)
    shard_rows = embed_table.shape[0]
    local_ids = every_id - vocab_index * shard_rows
    inside = (local_ids >= 0) & (local_ids < shard_rows)
    picked = jnp.take(embed_table, jnp.clip(local_ids, 0, shard_rows - 1).reshape(-1), axis=0)
    picked = picked.reshape(every_id.shape[0], every_id.shape[1], embed_table.shape[1])
    partial_rows = jnp.where(inside[:, :, None], picked, jnp.zeros_like(picked))
    arrived = lax.all_to_all(partial_rows, "seq", split_axis=1, concat_axis=2, tiled=True)
    summed = lax.psum(arrived.astype(jnp.float32).astype(jnp.bfloat16), "vocab").astype(jnp.float32)
    embedded_pairs = summed * keep_mask.astype(jnp.float32)[:, :, None]
    pair_count = embedded_pairs.shape[0]
    token_rows = embedded_pairs.shape[1]
    model_cols = embedded_pairs.shape[2]
    flat_rows = pair_count * token_rows
    embedded = embedded_pairs.reshape(flat_rows, model_cols)
    self_normed = rms_scale(embedded, self_gain).astype(jnp.bfloat16)
    queries = row_fold(self_normed, lax.all_gather(query_weight, "seq", axis=0, tiled=True))
    keys = row_fold(self_normed, lax.all_gather(key_weight, "seq", axis=0, tiled=True))
    values = row_fold(self_normed, lax.all_gather(value_weight, "seq", axis=0, tiled=True))
    head_cols = queries.shape[1]
    queries = queries.astype(jnp.bfloat16).reshape(pair_count, token_rows, head_cols)
    keys = keys.astype(jnp.bfloat16).reshape(pair_count, token_rows, head_cols)
    values = values.astype(jnp.bfloat16).reshape(pair_count, token_rows, head_cols)
    keys_every, values_every = (
        lax.all_gather(keys, "seq", axis=1, tiled=True),
        lax.all_gather(values, "seq", axis=1, tiled=True),
    )
    query_pos = seq_index * token_rows + jnp.arange(token_rows, dtype=jnp.int32)
    key_pos = jnp.arange(token_rows * seq_count, dtype=jnp.int32)
    causal = key_pos[None, :] <= query_pos[:, None]
    visible = causal[None, :, :] & (key_pos[None, None, :] < target_length[:, None, None])
    self_context = attend(queries, keys_every, values_every, visible).reshape(flat_rows, head_cols)
    self_terms = jnp.dot(self_context, self_out_weight, preferred_element_type=jnp.float32)
    share_cols = model_cols // vocab_count
    col_start = vocab_index * share_cols
    after_self = embedded + lax.psum(self_terms.astype(jnp.bfloat16), "vocab").astype(jnp.float32)
    cross_normed = rms_scale(after_self, cross_gain).astype(jnp.bfloat16)
    after_share = lax.dynamic_slice_in_dim(after_self, col_start, share_cols, 1)
    cross_queries = row_fold(
        cross_normed, lax.all_gather(cross_query_weight, "seq", axis=0, tiled=True)
    )
    cross_queries = cross_queries.astype(jnp.bfloat16).reshape(pair_count, token_rows, head_cols)
    source_keys, source_values = (
        lax.all_gather(cross_keys, "seq", axis=1, tiled=True),
        lax.all_gather(cross_values, "seq", axis=1, tiled=True),
    )
    source_pos = jnp.arange(source_keys.shape[1], dtype=jnp.int32)
    cross_visible = jnp.broadcast_to(
        source_pos[None, None, :] < source_length[:, None, None],
        (pair_count, token_rows, source_keys.shape[1]),
    )
    cross_context = attend(cross_queries, source_keys, source_values, cross_visible).reshape(
        flat_rows, head_cols
    )
    cross_terms = jnp.dot(cross_context, cross_out_weight, preferred_element_type=jnp.float32)
    cross_share = lax.psum_scatter(
        cross_terms.astype(jnp.bfloat16), "vocab", scatter_dimension=1, tiled=True
    ).astype(jnp.float32)
    return (
        (after_share + cross_share).reshape(pair_count, token_rows, share_cols).astype(jnp.bfloat16)
    )


def solution(mesh):
    return jax.shard_map(
        on_device,
        mesh=mesh,
        in_specs=(
            P(None, "seq"),
            P(None, "seq"),
            P(),
            P(),
            P("vocab", "seq"),
            P(),
            P("seq", "vocab"),
            P("seq", "vocab"),
            P("seq", "vocab"),
            P("vocab", None),
            P(),
            P("seq", "vocab"),
            P(None, "seq", "vocab"),
            P(None, "seq", "vocab"),
            P("vocab", None),
        ),
        out_specs=P(None, "seq", "vocab"),
        check_vma=False,
    )
```

profile of v0, /device:TPU:8, one launch (start us, length us, event | category | flops | bytes accessed | tf_op | source)
XLA Modules:
  0.0 1701.3 jit_solution(9061207319396813482)
XLA Ops:
  7.4 117.5 %all-gather = s32[32,64,2]{1,2,0:T(2,128)S(1)} all-gather(s32[1,64,2]{1,2,0:T(2,128)} %bitcast.79), channel_id=1, replica_groups=mesh['vocab'=16,'seq'=32] {'seq'}, dimensions={0}, use_global_device_ids=true | all-gather | bytes 16896 | tf_op jit(solution)/shard_map/all_gather | solution.py:56
  125.6 1.1 copy.49
  126.7 12.1 gather_fusion
  138.9 10.4 broadcast_select_fusion.1
  149.3 48.0 %all_to_all.18 = bf16[2,2048,128]{2,0,1:T(2,128)(2,1)S(1)} all-to-all(bf16[2,2048,128]{2,0,1:T(2,128)(2,1)S(1)} %broadcast_select_fusion.1), channel_id=1, replica_groups=mesh['vocab'=16,'seq'=32] {'seq'}, dimensions={1} | all-to-all | bytes 2097152 | tf_op jit(solution)/shard_map/all_to_all | solution.py:63
  197.3 0.7 copy.52
  198.0 1.3 all_to_all.16
  201.1 254.8 %all-reduce.3.cloned.1.call-done = bf16[2,64,4096]{2,1,0:T(8,128)(2,1)} async-done(((bf16[2,64,4096]{2,1,0:T(8,128)(2,1)}), bf16[2,64,4096]{2,1,0:T(8,128)(2,1)}) %all-reduce.3.cloned.1.call-update) | async-done | bytes 1048592 | tf_op jit(solution)/shard_map/psum | solution.py:64
  455.9 2.9 multiply_reduce_fusion.1
  458.8 1.9 fusion.1
  460.8 2.3 convolution_convert_fusion.3
  463.1 179.5 %all-gather.8.cloned.1.call-done = bf16[4096,128]{1,0:T(8,128)(2,1)} async-done(((bf16[128,128]{1,0:T(8,128)(2,1)}), bf16[4096,128]{1,0:T(8,128)(2,1)}) %all-gather.8.cloned.1.call-update) | async-done | bytes 1048592 | tf_op jit(solution)/shard_map/all_gather | solution.py:74
  642.6 2.3 convolution_convert_fusion.5
  645.4 219.1 %all-gather.12.cloned.1.call-done = bf16[4096,128]{1,0:T(8,128)(2,1)} async-done(((bf16[128,128]{1,0:T(8,128)(2,1)}), bf16[4096,128]{1,0:T(8,128)(2,1)}) %all-gather.12.cloned.1.call-update) | async-done | bytes 1048592 | tf_op jit(solution)/shard_map/all_gather | solution.py:72
  864.5 1.6 convolution_convert_fusion.4
  866.3 220.4 %all-gather.16.cloned.1.call-done = bf16[2,2048,128]{2,1,0:T(8,128)(2,1)} async-done(((bf16[2,64,128]{2,1,0:T(8,128)(2,1)}), bf16[2,2048,128]{2,1,0:T(8,128)(2,1)}) %all-gather.16.cloned.1.call-update) | async-done | bytes 1048592 | tf_op jit(solution)/shard_map/all_gather | solution.py:80
  1086.7 1.5 copy.54
  1088.8 1.3 copy-done.1
  1090.5 218.4 %all-gather.10.cloned.1.call-done = bf16[2,2048,128]{2,1,0:T(8,128)(2,1)} async-done(((bf16[2,64,128]{2,1,0:T(8,128)(2,1)}), bf16[2,2048,128]{2,1,0:T(8,128)(2,1)}) %all-gather.10.cloned.1.call-update) | async-done | bytes 1048592 | tf_op jit(solution)/shard_map/all_gather | solution.py:81
  1308.9 1.5 copy.53
  1310.4 2.1 fusion.7
  1312.7 2.6 convolution_convert_fusion.1
  1315.4 0.7 all-gather.18.cloned.1.call-update
  1316.2 116.6 %all_gather.34 = bf16[2,1024,128]{2,1,0:T(8,128)(2,1)S(1)} all-gather(bf16[2,32,128]{2,1,0:T(8,128)(2,1)S(1)} %copy-done.6), channel_id=1, replica_groups=mesh['vocab'=16,'seq'=32] {'seq'}, dimensions={1}, use_global_device_ids=true | all-gather | bytes 540672 | tf_op jit(solution)/shard_map/all_gather | solution.py:99
  1433.0 123.8 %all_gather.35 = bf16[2,1024,128]{2,1,0:T(8,128)(2,1)S(1)} all-gather(bf16[2,32,128]{2,1,0:T(8,128)(2,1)S(1)} %copy-done.7), channel_id=1, replica_groups=mesh['vocab'=16,'seq'=32] {'seq'}, dimensions={1}, use_global_device_ids=true | all-gather | bytes 540672 | tf_op jit(solution)/shard_map/all_gather | solution.py:100
  1556.8 1.0 copy.59
  1557.9 17.1 %all-reduce.5.cloned.1.call-done = bf16[128,4096]{1,0:T(8,128)(2,1)} async-done(((bf16[128,4096]{1,0:T(8,128)(2,1)}), bf16[128,4096]{1,0:T(8,128)(2,1)}) %all-reduce.5.cloned.1.call-update) | async-done | bytes 1048592 | tf_op jit(solution)/shard_map/psum | solution.py:91
  1575.0 3.5 multiply_reduce_fusion
  1578.6 2.3 convolution_convert_fusion.2
  1582.7 1.4 convolution_convert_fusion
  1584.1 108.5 %reduce-scatter.2.cloned.1.call-done = bf16[128,256]{1,0:T(8,128)(2,1)} async-done(((bf16[128,4096]{1,0:T(8,128)(2,1)}), bf16[128,256]{1,0:T(8,128)(2,1)}) %reduce-scatter.2.cloned.1.call-update) | async-done | bytes 65552 | tf_op jit(solution)/shard_map/reduce_scatter | solution.py:111
  1692.6 1.6 add_convert_fusion
  (70 shorter events, 6.6 us)
Async XLA Ops:
  7.4 119.4 %copy-start = (bf16[8192,128]{1,0:T(8,128)(2,1)S(1)}, bf16[8192,128]{1,0:T(8,128)(2,1)}, u32[]{:S(2)}) copy-start(bf16[8192,128]{1,0:T(8,128)(2,1)} %param.19) | copy-start | bytes 6291460
  7.4 448.5 %all-reduce.3.cloned.1.call-start = ((), (), s32[]{:S(2)}) async-start(), calls=%async_computation.2 | async-start | bytes 2097152 | tf_op jit(solution)/shard_map/psum | solution.py:64
  198.0 3.1 copy-start.8
  199.2 259.6 %copy-start.4 = (f32[4096]{0:T(1024)S(1)}, f32[4096]{0:T(1024)}, u32[]{:S(2)}) copy-start(f32[4096]{0:T(1024)} %param.20) | copy-start | bytes 49156
  199.3 261.5 %all-gather.14.cloned.1.call-start = ((), (), s32[]{:S(2)}) async-start(), calls=%async_computation.6 | async-start | bytes 1081344 | tf_op jit(solution)/shard_map/all_gather | solution.py:73
  199.9 442.8 %all-gather.8.cloned.1.call-start = ((), (), s32[]{:S(2)}) async-start(), calls=%async_computation.3 | async-start | bytes 1081344 | tf_op jit(solution)/shard_map/all_gather | solution.py:74
  200.4 664.1 %all-gather.12.cloned.1.call-start = ((), (), s32[]{:S(2)}) async-start(), calls=%async_computation.5 | async-start | bytes 1081344 | tf_op jit(solution)/shard_map/all_gather | solution.py:72
  201.0 885.7 %all-gather.16.cloned.1.call-start = ((), (), s32[]{:S(2)}) async-start(), calls=%async_computation.7 | async-start | bytes 1081344 | tf_op jit(solution)/shard_map/all_gather | solution.py:80
  460.7 184.3 %copy-start.9 = (s32[2]{0:T(128)S(1)}, s32[2]{0:T(128)}, u32[]{:S(2)}) copy-start(s32[2]{0:T(128)} %param.17) | copy-start | bytes 28
  463.0 845.8 %all-gather.10.cloned.1.call-start = ((), (), s32[]{:S(2)}) async-start(), calls=%async_computation.4 | async-start | bytes 1081344 | tf_op jit(solution)/shard_map/all_gather | solution.py:81
  644.9 930.1 %all-reduce.5.cloned.1.call-start = ((), (), s32[]{:S(2)}) async-start(), calls=%async_computation.8 | async-start | bytes 2097152 | tf_op jit(solution)/shard_map/psum | solution.py:91
  1088.8 1.3 copy-start.1
  1312.5 3.7 copy-start.6
  1312.7 120.3 %copy-start.7 = (bf16[2,32,128]{2,1,0:T(8,128)(2,1)S(1)}, bf16[2,32,128]{2,1,0:T(8,128)(2,1)}, u32[]{:S(2)}) copy-start(bf16[2,32,128]{2,1,0:T(8,128)(2,1)} %param.28) | copy-start | bytes 49156
  1315.4 242.5 %copy-start.10 = (s32[2]{0:T(128)S(1)}, s32[2]{0:T(128)}, u32[]{:S(2)}) copy-start(s32[2]{0:T(128)} %param.18) | copy-start | bytes 28
  1315.4 263.2 %all-gather.18.cloned.1.call-start = ((), (), s32[]{:S(2)}) async-start(), calls=%async_computation.9 | async-start | bytes 1081344 | tf_op jit(solution)/shard_map/all_gather | solution.py:95
  1316.1 376.5 %reduce-scatter.2.cloned.1.call-start = ((), (), s32[]{:S(2)}) async-start(), calls=%async_computation.10 | async-start | bytes 1114112 | tf_op jit(solution)/shard_map/reduce_scatter | solution.py:111
  1557.9 20.6 %copy-start.5 = (f32[4096]{0:T(1024)S(1)}, f32[4096]{0:T(1024)}, u32[]{:S(2)}) copy-start(f32[4096]{0:T(1024)} %param.25) | copy-start | bytes 49156
  1581.0 1.0 copy-start.3
  1581.4 1.3 copy-start.2
Sparse Core Ops, SparseCore 0:
  199.4 256.4 all-reduce.2
  1315.5 259.4 all-reduce.4
  1584.2 108.3 reduce-scatter.1
Sparse Core Ops, SparseCore 1:
  201.8 219.4 all-gather.13
  423.3 219.3 all-gather.7
  644.6 219.9 all-gather.11
  866.6 220.0 all-gather.15
  1088.8 220.0 all-gather.9
  1318.2 220.8 all-gather.17
where the time goes:
time: 1700 us
  waiting for transfers between devices  1220 us (72%)
  blocking collectives  406 us (24%)
  local copies, waits for them, and re-layouts  22.4 us (1%)
  other arithmetic  21.6 us (1%)
    psum x1, waiting for transfers between devices, on_device(): lax.psum(arrived.astype(jnp.float32).astype(jnp.bfloat16), 'vocab')  255 us
    all_gather x1, waiting for transfers between devices, on_device(): lax.all_gather(keys, 'seq', axis=1, tiled=True)  220 us
    all_gather x1, waiting for transfers between devices, on_device(): lax.all_gather(query_weight, 'seq', axis=0, tiled=True)  219 us
    all_gather x1, waiting for transfers between devices, on_device(): lax.all_gather(values, 'seq', axis=1, tiled=True)  218 us
    all_gather x1, waiting for transfers between devices, on_device(): lax.all_gather(value_weight, 'seq', axis=0, tiled=True)  180 us
    all_gather x1, blocking collectives, on_device(): lax.all_gather(cross_values, 'seq', axis=1, tiled=True)  124 us
    all_gather x1, blocking collectives, on_device(): every_id = lax.all_gather(token_ids, 'seq', axis=1, tiled=True)  117 us
    all_gather x1, blocking collectives, on_device(): lax.all_gather(cross_keys, 'seq', axis=1, tiled=True)  117 us
  transfers between devices with their start and end apart: 9, of which 7 were waited for; matrix products, arithmetic and copies ran while one was open for 1% of the time, Pallas kernels for 0%

commit v1 on v0

--- a/solution.py
+++ b/solution.py
@@ -61,7 +61,9 @@
     picked = picked.reshape(every_id.shape[0], every_id.shape[1], embed_table.shape[1])
     partial_rows = jnp.where(inside[:, :, None], picked, jnp.zeros_like(picked))
     arrived = lax.all_to_all(partial_rows, "seq", split_axis=1, concat_axis=2, tiled=True)
-    summed = lax.psum(arrived.astype(jnp.float32).astype(jnp.bfloat16), "vocab").astype(jnp.float32)
+    summed = jnp.sum(
+        lax.all_gather(arrived.astype(jnp.float32).astype(jnp.bfloat16), "vocab"), axis=0
+    ).astype(jnp.float32)
     embedded_pairs = summed * keep_mask.astype(jnp.float32)[:, :, None]
     pair_count = embedded_pairs.shape[0]
     token_rows = embedded_pairs.shape[1]

time: 1700 us -> 2210 us (1.30)
  waiting for transfers between devices: 1220 us -> 1710 us
    all_gather x0 -> x1, waiting for transfers between devices: none -> 279 us  [on_device(): lax.all_gather(arrived.astype(jnp.float32).astype(jnp.bfloat16), 'vocab')]
    psum x1 -> x0, waiting for transfers between devices: 255 us -> none  [on_device(): lax.psum(arrived.astype(jnp.float32).astype(jnp.bfloat16), 'vocab')]
    all_gather x1, waiting for transfers between devices: 0.03 us -> 223 us  [on_device(): lax.all_gather(key_weight, 'seq', axis=0, tiled=True)]
    all_gather x1, waiting for transfers between devices: 0.01 us -> 221 us  [on_device(): lax.all_gather(cross_query_weight, 'seq', axis=0, tiled=True)]
    all_gather x1, waiting for transfers between devices: 180 us -> 219 us  [on_device(): lax.all_gather(value_weight, 'seq', axis=0, tiled=True)]
  transfers between devices with their start and end apart: 9 -> 9, of which waited for: 7 -> 9; matrix products, arithmetic and copies ran while one was open for 1% -> 1% of each run, Pallas kernels for 0% -> 0%
where the time goes in v1:
time: 2210 us
  waiting for transfers between devices  1710 us (77%)
  blocking collectives  415 us (19%)
  local copies, waits for them, and re-layouts  27.1 us (1%)
  other arithmetic  27.1 us (1%)
    all_gather x1, waiting for transfers between devices, on_device(): lax.all_gather(arrived.astype(jnp.float32).astype(jnp.bfloat16), 'vocab')  279 us
    all_gather x1, waiting for transfers between devices, on_device(): lax.all_gather(key_weight, 'seq', axis=0, tiled=True)  223 us
    all_gather x1, waiting for transfers between devices, on_device(): lax.all_gather(cross_query_weight, 'seq', axis=0, tiled=True)  221 us
    all_gather x1, waiting for transfers between devices, on_device(): lax.all_gather(keys, 'seq', axis=1, tiled=True)  220 us
    all_gather x1, waiting for transfers between devices, on_device(): lax.all_gather(value_weight, 'seq', axis=0, tiled=True)  219 us
    all_gather x1, waiting for transfers between devices, on_device(): lax.all_gather(query_weight, 'seq', axis=0, tiled=True)  219 us
    all_gather x1, waiting for transfers between devices, on_device(): lax.all_gather(values, 'seq', axis=1, tiled=True)  216 us
    all_gather x1, blocking collectives, on_device(): lax.all_gather(cross_values, 'seq', axis=1, tiled=True)  128 us
  transfers between devices with their start and end apart: 9, of which 9 were waited for; matrix products, arithmetic and copies ran while one was open for 1% of the time, Pallas kernels for 0%

profile of v1, /device:TPU:8, one launch (start us, length us, event | category | flops | bytes accessed | tf_op | source)
XLA Modules:
  0.0 2211.2 jit_solution(13283011538942241518)
XLA Ops:
  6.5 117.5 %all-gather = s32[32,64,2]{1,2,0:T(2,128)S(1)} all-gather(s32[1,64,2]{1,2,0:T(2,128)} %bitcast.78), channel_id=1, replica_groups=mesh['vocab'=16,'seq'=32] {'seq'}, dimensions={0}, use_global_device_ids=true | all-gather | bytes 16896 | tf_op jit(solution)/shard_map/all_gather | solution.py:56
  125.9 12.1 gather_fusion
  138.0 10.4 broadcast_select_fusion.1
  148.5 48.0 %all_to_all.15 = bf16[2,2048,128]{2,0,1:T(2,128)(2,1)S(1)} all-to-all(bf16[2,2048,128]{2,0,1:T(2,128)(2,1)S(1)} %broadcast_select_fusion.1), channel_id=1, replica_groups=mesh['vocab'=16,'seq'=32] {'seq'}, dimensions={1} | all-to-all | bytes 2097152 | tf_op jit(solution)/shard_map/all_to_all | solution.py:63
  200.8 278.7 %all-gather.9.cloned.1.call-done = bf16[16,2,64,4096]{3,2,1,0:T(8,128)(2,1)} async-done(((bf16[1,2,64,4096]{3,2,1,0:T(8,128)(2,1)}), bf16[16,2,64,4096]{3,2,1,0:T(8,128)(2,1)}) %all-gather.9.cloned.1.call-update) | async-done | bytes 16777232 | tf_op jit(solution)/shard_map/all_gather | solution.py:65
  479.5 8.9 reduce_sum.48
  489.0 1.4 multiply_convert_fusion.1
  490.4 222.7 %all-gather.17.cloned.1.call-done = bf16[4096,128]{1,0:T(8,128)(2,1)} async-done(((bf16[128,128]{1,0:T(8,128)(2,1)}), bf16[4096,128]{1,0:T(8,128)(2,1)}) %all-gather.17.cloned.1.call-update) | async-done | bytes 1048592 | tf_op jit(solution)/shard_map/all_gather | solution.py:75
  713.1 2.6 convolution_convert_fusion.3
  715.7 219.4 %all-gather.11.cloned.1.call-done = bf16[4096,128]{1,0:T(8,128)(2,1)} async-done(((bf16[128,128]{1,0:T(8,128)(2,1)}), bf16[4096,128]{1,0:T(8,128)(2,1)}) %all-gather.11.cloned.1.call-update) | async-done | bytes 1048592 | tf_op jit(solution)/shard_map/all_gather | solution.py:76
  935.1 2.6 convolution_convert_fusion.5
  938.2 218.8 %all-gather.15.cloned.1.call-done = bf16[4096,128]{1,0:T(8,128)(2,1)} async-done(((bf16[128,128]{1,0:T(8,128)(2,1)}), bf16[4096,128]{1,0:T(8,128)(2,1)}) %all-gather.15.cloned.1.call-update) | async-done | bytes 1048592 | tf_op jit(solution)/shard_map/all_gather | solution.py:74
  1157.0 2.0 convolution_convert_fusion.4
  1159.1 220.0 %all-gather.19.cloned.1.call-done = bf16[2,2048,128]{2,1,0:T(8,128)(2,1)} async-done(((bf16[2,64,128]{2,1,0:T(8,128)(2,1)}), bf16[2,2048,128]{2,1,0:T(8,128)(2,1)}) %all-gather.19.cloned.1.call-update) | async-done | bytes 1048592 | tf_op jit(solution)/shard_map/all_gather | solution.py:82
  1379.1 2.3 copy.65
  1381.4 1.8 fusion.17
  1383.2 1.3 copy-done.1
  1384.9 216.1 %all-gather.13.cloned.1.call-done = bf16[2,2048,128]{2,1,0:T(8,128)(2,1)} async-done(((bf16[2,64,128]{2,1,0:T(8,128)(2,1)}), bf16[2,2048,128]{2,1,0:T(8,128)(2,1)}) %all-gather.13.cloned.1.call-update) | async-done | bytes 1048592 | tf_op jit(solution)/shard_map/all_gather | solution.py:83
  1601.1 2.3 copy.64
  1603.3 2.4 fusion.5
  1606.0 2.6 convolution_convert_fusion.1
  1609.5 121.2 %all_gather.42 = bf16[2,1024,128]{2,1,0:T(8,128)(2,1)} all-gather(bf16[2,32,128]{2,1,0:T(8,128)(2,1)S(1)} %copy-done.7), channel_id=1, replica_groups=mesh['vocab'=16,'seq'=32] {'seq'}, dimensions={1}, use_global_device_ids=true | all-gather | bytes 540672 | tf_op jit(solution)/shard_map/all_gather | solution.py:101
  1730.7 2.0 copy.68
  1732.7 128.4 %all_gather.43 = bf16[2,1024,128]{2,1,0:T(8,128)(2,1)} all-gather(bf16[2,32,128]{2,1,0:T(8,128)(2,1)S(1)} %copy-done.8), channel_id=1, replica_groups=mesh['vocab'=16,'seq'=32] {'seq'}, dimensions={1}, use_global_device_ids=true | all-gather | bytes 540672 | tf_op jit(solution)/shard_map/all_gather | solution.py:102
  1861.2 2.1 copy.70
  1863.3 3.7 all-reduce.2.cloned.1.call-done
  1867.0 3.0 multiply_reduce_fusion
  1870.0 221.3 %all-gather.21.cloned.1.call-done = bf16[4096,128]{1,0:T(8,128)(2,1)} async-done(((bf16[128,128]{1,0:T(8,128)(2,1)}), bf16[4096,128]{1,0:T(8,128)(2,1)}) %all-gather.21.cloned.1.call-update) | async-done | bytes 1048592 | tf_op jit(solution)/shard_map/all_gather | solution.py:97
  2091.4 2.3 convolution_convert_fusion.2
  2095.4 1.4 convolution_convert_fusion
  2096.9 106.2 %reduce-scatter.2.cloned.1.call-done = bf16[128,256]{1,0:T(8,128)(2,1)} async-done(((bf16[128,4096]{1,0:T(8,128)(2,1)}), bf16[128,256]{1,0:T(8,128)(2,1)}) %reduce-scatter.2.cloned.1.call-update) | async-done | bytes 65552 | tf_op jit(solution)/shard_map/reduce_scatter | solution.py:113
  2203.0 1.6 add_convert_fusion
  (75 shorter events, 10.5 us)
Async XLA Ops:
  6.5 119.4 %copy-start = (bf16[8192,128]{1,0:T(8,128)(2,1)S(1)}, bf16[8192,128]{1,0:T(8,128)(2,1)}, u32[]{:S(2)}) copy-start(bf16[8192,128]{1,0:T(8,128)(2,1)} %param.19) | copy-start | bytes 6291460
  6.5 472.9 %all-gather.9.cloned.1.call-start = ((), (), s32[]{:S(2)}) async-start(), calls=%async_computation.2 | async-start | bytes 17825792 | tf_op jit(solution)/shard_map/all_gather | solution.py:65
  197.3 3.4 copy-start.9
  198.6 514.5 %all-gather.17.cloned.1.call-start = ((), (), s32[]{:S(2)}) async-start(), calls=%async_computation.6 | async-start | bytes 1081344 | tf_op jit(solution)/shard_map/all_gather | solution.py:75
  199.3 735.8 %all-gather.11.cloned.1.call-start = ((), (), s32[]{:S(2)}) async-start(), calls=%async_computation.3 | async-start | bytes 1081344 | tf_op jit(solution)/shard_map/all_gather | solution.py:76
  200.1 957.0 %all-gather.15.cloned.1.call-start = ((), (), s32[]{:S(2)}) async-start(), calls=%async_computation.5 | async-start | bytes 1081344 | tf_op jit(solution)/shard_map/all_gather | solution.py:74
  200.6 1178.4 %all-gather.19.cloned.1.call-start = ((), (), s32[]{:S(2)}) async-start(), calls=%async_computation.7 | async-start | bytes 1081344 | tf_op jit(solution)/shard_map/all_gather | solution.py:82
  200.8 288.2 %copy-start.5 = (f32[4096]{0:T(1024)S(1)}, f32[4096]{0:T(1024)}, u32[]{:S(2)}) copy-start(f32[4096]{0:T(1024)} %param.20) | copy-start | bytes 49156
  490.4 447.4 %copy-start.10 = (s32[2]{0:T(128)S(1)}, s32[2]{0:T(128)}, u32[]{:S(2)}) copy-start(s32[2]{0:T(128)} %param.17) | copy-start | bytes 28
  715.7 885.4 %all-gather.13.cloned.1.call-start = ((), (), s32[]{:S(2)}) async-start(), calls=%async_computation.4 | async-start | bytes 1081344 | tf_op jit(solution)/shard_map/all_gather | solution.py:83
  937.7 929.2 %all-reduce.2.cloned.1.call-start = ((), (), s32[]{:S(2)}) async-start(), calls=%async_computation.8 | async-start | bytes 2097152 | tf_op jit(solution)/shard_map/psum | solution.py:93
  1383.2 1.3 copy-start.1
  1605.8 3.7 copy-start.7
  1606.0 126.7 %copy-start.8 = (bf16[2,32,128]{2,1,0:T(8,128)(2,1)S(1)}, bf16[2,32,128]{2,1,0:T(8,128)(2,1)}, u32[]{:S(2)}) copy-start(bf16[2,32,128]{2,1,0:T(8,128)(2,1)} %param.28) | copy-start | bytes 49156
  1608.6 254.6 %copy-start.11 = (s32[2]{0:T(128)S(1)}, s32[2]{0:T(128)}, u32[]{:S(2)}) copy-start(s32[2]{0:T(128)} %param.18) | copy-start | bytes 28
  1608.7 482.7 %all-gather.21.cloned.1.call-start = ((), (), s32[]{:S(2)}) async-start(), calls=%async_computation.9 | async-start | bytes 1081344 | tf_op jit(solution)/shard_map/all_gather | solution.py:97
  1609.4 593.6 %reduce-scatter.2.cloned.1.call-start = ((), (), s32[]{:S(2)}) async-start(), calls=%async_computation.10 | async-start | bytes 1114112 | tf_op jit(solution)/shard_map/reduce_scatter | solution.py:113
  1863.3 228.1 %copy-start.6 = (f32[4096]{0:T(1024)S(1)}, f32[4096]{0:T(1024)}, u32[]{:S(2)}) copy-start(f32[4096]{0:T(1024)} %param.25) | copy-start | bytes 49156
  1870.0 223.8 %copy-start.2 = (bf16[2,1024,128]{1,2,0:T(8,128)(2,1)S(1)}, bf16[2,1024,128]{1,2,0:T(8,128)(2,1)}, u32[]{:S(2)}) copy-start(bf16[2,1024,128]{1,2,0:T(8,128)(2,1)} %copy.68) | copy-start | bytes 1572868
  2093.8 1.0 copy-start.4
  2094.2 1.3 copy-start.3
Sparse Core Ops, SparseCore 0:
  198.7 280.7 all-gather.8
  481.6 231.4 all-gather.16
  715.2 219.9 all-gather.10
  937.1 219.9 all-gather.14
  1159.0 220.0 all-gather.18
  1381.0 220.0 all-gather.12
  1608.8 258.1 all-reduce.1
  1869.1 222.2 all-gather.20
  2097.0 106.0 reduce-scatter.1
